TPU v7x, 32 devices: a whole 2x2x4 slice. The times are simulated.
32 devices in a mesh: qubit: 16 (over z, x, core), head: 2 (over y).
Axes of the slice: x: 2, y: 2, z: 4, core: 2. Of those that a mesh axis runs over, the one named last changes fastest.
Arguments:
- tokens: bfloat16 [128, 256, 512], P('qubit'), may hold values from -6 to 6
- kv_cache: bfloat16 [128, 8, 384, 128], P('qubit', 'head'), may hold values from -6 to 6
- cache_age: int32 [128, 3], P('qubit'), may hold values from 1 to 8
- partner: int32 [128], P('qubit'), may hold values from 0 to 127, as said below
- slope: float32 [8], P('head'), may hold values from 0.03 to 1.5
- w_qkv: bfloat16 [3, 512, 512], P(None, None, 'head'), may hold values from -0.25 to 0.25
- w_o: bfloat16 [512, 512], replicated, may hold values from -0.25 to 0.25
- attn_gain: float32 [512], replicated, may hold values from 0.5 to 1.5
- mlp_gain: float32 [512], replicated, may hold values from 0.5 to 1.5
- w_in: bfloat16 [512, 2048], P(None, 'head'), may hold values from -0.25 to 0.25
- w_down: bfloat16 [2048, 512], P('head'), may hold values from -0.125 to 0.125
Outputs:
- decoded: bfloat16 [128, 256, 512], P('qubit', 'head')
Inputs may be any that keep to these rules, and one draw needn't show every extreme that they name: partner pairs the qubits: partner[partner[q]] = q. With H = 8, the 8 qubits of device d (q // 8 = d) carry the colours 0 to 7, one each, in an order drawn per device; the qubit of colour c pairs with the qubit of colour c on device H + (d + c) mod H if d < H, on device (d - H - c) mod H if d >= H.
All inputs are finite; a program needn't handle non-finite values.
Results may differ from a plain program's by a relative error of at most 0.0065.
Values may be sent and summed in bfloat16 or wider, within the bound.
A program may use at most 128 MiB of HBM per device.

v0:
```python
import functools

import jax
import jax.numpy as jnp
from jax import lax
from jax.experimental import pallas as pl
from jax.experimental.pallas import tpu as pltpu
from jax.sharding import PartitionSpec as P

DH = 64
STAB = 128
PARTS = 3
F32 = jnp.float32
BF16 = jnp.bfloat16
MESH = pl.DeviceIdType.MESH
VMEM_BYTES = 67043328
ANY_SPEC = pl.BlockSpec(memory_space=pl.ANY)
SMEM_SPEC = pl.BlockSpec(memory_space=pltpu.SMEM)
VMEM_SPEC = pl.BlockSpec(memory_space=pltpu.VMEM)


def mm(a, b):
    return jnp.dot(a, b, preferred_element_type=F32)


def rms(x, gain):
    return x * lax.rsqrt(jnp.mean(x * x, axis=-1, keepdims=True) + 1e-06) * gain


def head_attention(queries, parts):
    tokens = queries.shape[0]
    blocks, tops = [], []
    for keys, _, biases, firsts in parts:
        s = lax.dot_general(keys, queries, (((1,), (1,)), ((), ())), preferred_element_type=F32)
        for i, (bias, first) in enumerate(zip(biases, firsts)):
            block = s[i * STAB : (i + 1) * STAB, first:]
            top = jnp.max(block, axis=0, keepdims=True) + bias
            if first:
                top = jnp.concatenate([jnp.full((1, first), -1e30, F32), top], axis=1)
            blocks.append((block, bias, first))
            tops.append(top)
    top = functools.reduce(jnp.maximum, tops)
    weights, total = [], None
    for block, bias, first in blocks:
        w = jnp.exp(block + (bias - top[:, first:]))
        if first:
            w = jnp.concatenate([jnp.zeros((STAB, first), F32), w], axis=1)
        weights.append(w.astype(BF16))
        total = w if total is None else total + w
    total = jnp.sum(total, axis=0, keepdims=True)
    at, summed = 0, None
    for _, values, biases, _ in parts:
        w = jnp.concatenate(weights[at : at + len(biases)], axis=0)
        at += len(biases)
        term = lax.dot_general(values, w, (((0,), (0,)), ((), ())), preferred_element_type=F32)
        summed = term if summed is None else summed + term
    return summed / total, top + jnp.log(total)


def layer_kernel(
    n_dev,
    partner_ref,
    age_ref,
    slope_ref,
    tokens_hbm,
    cache_hbm,
    w_qkv_hbm,
    w_o_hbm,
    gain1_ref,
    gain2_ref,
    w_in_hbm,
    w_down_hbm,
    out_ref,
    order,
    colour,
    tok,
    cache,
    w_qkv,
    w_o,
    w_in,
    w_dn,
    normed,
    q_send,
    q_recv,
    n_send,
    n_all,
    f_send,
    f_recv,
    result,
    lse_scr,
    load_sem,
    w_ss,
    w_rs,
    q_ss,
    q_rs,
    n_ss,
    n_rs,
    f_ss,
    f_rs,
):
    count, new_len, _ = tok.shape
    heads, keys = cache.shape[1], cache.shape[2]
    hd = heads * DH
    rounds, new_rounds = keys // STAB, new_len // STAB
    rows = out_ref.shape[1]
    half = n_dev // 2
    me = lax.axis_index("qubit").astype(jnp.int32)
    y = lax.axis_index("head").astype(jnp.int32)
    n = n_all.shape[1]

    def beside(r):
        return lax.rem(y + r, n)

    def mate(c):
        return jnp.where(me < half, half + lax.rem(me + c, half), lax.rem(me - c + 2 * half, half))

    def load(i, src, dst):
        return pltpu.make_async_copy(src, dst, load_sem.at[i])

    first_loads = [load(0, tokens_hbm, tok), load(1, w_qkv_hbm, w_qkv)]
    later_loads = [
        load(2, cache_hbm, cache),
        load(3, w_o_hbm, w_o),
        load(4, w_in_hbm, w_in.at[0]),
        load(5, w_down_hbm, w_dn.at[0]),
    ]
    for copy in first_loads:
        copy.start()

    barrier = pltpu.get_barrier_semaphore()
    for c in range(count):
        for t in range(n):
            pl.semaphore_signal(barrier, inc=1, device_id=(mate(c), t), device_id_type=MESH)
    for r in range(1, n):
        pl.semaphore_signal(barrier, inc=1, device_id=(me, beside(r)), device_id_type=MESH)

    tints = []
    for q in range(count):
        owner = lax.div(partner_ref[q], count)
        tints.append(jnp.where(me < half, lax.rem(owner - me + n_dev, half), lax.rem(me - owner + n_dev, half)))
        colour[q] = jnp.minimum(tints[q], count - 1)
    for c in range(count):
        order[c] = functools.reduce(jnp.maximum, [jnp.where(tint == c, q, 0) for q, tint in enumerate(tints)])
    lse_scr[...] = jnp.zeros_like(lse_scr)

    def q_copy(c):
        return pltpu.make_async_remote_copy(
            src_ref=q_send.at[c],
            dst_ref=q_recv.at[c],
            send_sem=q_ss.at[c],
            recv_sem=q_rs.at[c],
            device_id=(mate(c), y),
            device_id_type=MESH,
        )

    def n_copy(c, r):
        return pltpu.make_async_remote_copy(
            src_ref=n_send.at[c, beside(r)],
            dst_ref=n_all.at[c, y],
            send_sem=n_ss.at[c, r],
            recv_sem=n_rs.at[c, y],
            device_id=(me, beside(r)),
            device_id_type=MESH,
        )

    def n_arrival(c, r):
        group = beside(n - r)
        return pltpu.make_async_remote_copy(
            src_ref=n_send.at[c, group],
            dst_ref=n_all.at[c, group],
            send_sem=n_ss.at[c, r],
            recv_sem=n_rs.at[c, group],
            device_id=(me, group),
            device_id_type=MESH,
        )

    def f_copy(c, t):
        return pltpu.make_async_remote_copy(
            src_ref=f_send.at[c, t],
            dst_ref=f_recv.at[c, y],
            send_sem=f_ss.at[c, t],
            recv_sem=f_rs.at[c, y],
            device_id=(mate(c), t),
            device_id_type=MESH,
        )

    def f_arrival(c, group):
        return pltpu.make_async_remote_copy(
            src_ref=f_send.at[c, 0],
            dst_ref=f_recv.at[c, group],
            send_sem=f_ss.at[c, 0],
            recv_sem=f_rs.at[c, group],
            device_id=(mate(c), group),
            device_id_type=MESH,
        )

    def w_copy(i, r, src, dst):
        return pltpu.make_async_remote_copy(
            src_ref=src,
            dst_ref=dst.at[r],
            send_sem=w_ss.at[i, r],
            recv_sem=w_rs.at[i, r],
            device_id=(me, beside(r)),
            device_id_type=MESH,
        )

    w_copies = []
    for r in range(1, n):
        w_copies += [w_copy(0, r, w_in_hbm, w_in), w_copy(1, r, w_down_hbm, w_dn)]

    def project(c):
        x = rms(tok[order[c]].astype(F32), gain1_ref[...]).astype(BF16)
        normed[c] = x
        q_send[c] = (mm(x, w_qkv[0]).astype(BF16) * jnp.asarray(DH**-0.5, BF16)).astype(BF16)

    for copy in first_loads:
        copy.wait()
    project(0)
    for copy in later_loads:
        copy.start()
    project(1)
    pl.semaphore_wait(barrier, n * count + n - 1)

    def send_loop(c, _):
        q_copy(c - 2).start()
        project(c)
        return 0

    lax.fori_loop(2, count, send_loop, 0)
    q_copy(count - 2).start()
    q_copy(count - 1).start()
    for copy in w_copies:
        copy.start()
    later_loads[0].wait()

    def cache_part(row, h):
        kv = cache[row, h]
        biases = [-slope_ref[h] * age_ref[row, r].astype(F32) for r in range(rounds)]
        return kv[:, :DH], kv[:, DH:], biases, [0] * rounds

    def note_lse(h, lse):
        for p in range(PARTS):
            part = lse.astype(BF16).astype(F32)
            lse_scr[p * heads + h : p * heads + h + 1, :] = part
            lse = lse - part

    def put(buffer, c, at, value):
        value = value.astype(BF16)
        for t in range(n):
            buffer[c, t, at, :] = value[:, t * rows : (t + 1) * rows]

    def near(c):
        row = order[c]
        x = normed[c]
        k = mm(x, w_qkv[1]).astype(BF16)
        v = mm(x, w_qkv[2]).astype(BF16)
        for h in range(heads):
            cols = slice(h * DH, (h + 1) * DH)
            slope = slope_ref[h]
            fresh = (
                k[:, cols],
                v[:, cols],
                [slope * float(r) for r in range(new_rounds)],
                [r * STAB for r in range(new_rounds)],
            )
            out, lse = head_attention(q_send[c, :, cols], [cache_part(row, h), fresh])
            put(n_send, c, cols, out)
            note_lse(h, lse)
        put(n_send, c, slice(hd, None), lse_scr[...])
        n_all[c, y] = n_send[c, y]

    def far(c):
        row = order[c]
        for h in range(heads):
            cols = slice(h * DH, (h + 1) * DH)
            out, lse = head_attention(q_recv[c, :, cols], [cache_part(row, h)])
            put(f_send, c, cols, out)
            note_lse(h, lse)
        put(f_send, c, slice(hd, None), lse_scr[...])

    def attend_loop(c, _):
        near(c)
        for r in range(1, n):
            n_copy(c, r).start()
        q_copy(c).wait_recv()
        far(c)
        for t in range(n):
            f_copy(c, t).start()
        return 0

    lax.fori_loop(0, count, attend_loop, 0)

    for copy in later_loads[1:]:
        copy.wait()
    for copy in w_copies:
        copy.wait()

    def lse_of(tile):
        tail = tile[hd:, :].astype(F32)
        return sum(tail[p * heads : (p + 1) * heads] for p in range(PARTS))

    def finish_loop(c, _):
        for r in range(1, n):
            n_arrival(c, r).wait_recv()
        feats = []
        for group in range(n):
            f_arrival(c, group).wait_recv()
            near_part, far_part = n_all[c, group], f_recv[c, group]
            lse_near, lse_far = lse_of(near_part), lse_of(far_part)
            top = jnp.maximum(lse_near, lse_far)
            a, b = jnp.exp(lse_near - top), jnp.exp(lse_far - top)
            a, b = a / (a + b), b / (a + b)
            for h in range(heads):
                cols = slice(h * DH, (h + 1) * DH)
                feats.append(
                    near_part[cols].astype(F32) * a[h : h + 1] + far_part[cols].astype(F32) * b[h : h + 1]
                )
        attended = jnp.transpose(jnp.concatenate(feats, axis=0)).astype(BF16)
        x = tok[order[c], pl.ds(pl.multiple_of(y * rows, rows), rows), :].astype(F32)
        hidden = x + mm(attended, w_o[...])
        mlp_in = rms(hidden, gain2_ref[...]).astype(BF16)
        total = hidden
        for r in range(n):
            total = total + mm(jax.nn.gelu(mm(mlp_in, w_in[r])).astype(BF16), w_dn[r])
        result[c] = total.astype(BF16)
        return 0

    lax.fori_loop(0, count, finish_loop, 0)
    for q in range(count):
        out_ref[q] = result[colour[q]]

    def drain_loop(c, _):
        q_copy(c).wait_send()
        for r in range(1, n):
            n_copy(c, r).wait_send()
        for t in range(n):
            f_copy(c, t).wait_send()
        return 0

    lax.fori_loop(0, count, drain_loop, 0)


def on_device(n_dev, n, tokens, kv_cache, cache_age, partner, slope, w_qkv, w_o, attn_gain, mlp_gain, w_in, w_down):
    count, new_len, width = tokens.shape
    heads = kv_cache.shape[1]
    hd = heads * DH
    rows = new_len // n
    tall = hd + 16
    dma = pltpu.SemaphoreType.DMA
    return pl.pallas_call(
        functools.partial(layer_kernel, n_dev),
        in_specs=[SMEM_SPEC] * 3 + [ANY_SPEC] * 4 + [VMEM_SPEC] * 2 + [ANY_SPEC] * 2,
        out_specs=VMEM_SPEC,
        out_shape=jax.ShapeDtypeStruct((count, rows, width), BF16),
        scratch_shapes=[
            pltpu.SMEM((count,), jnp.int32),
            pltpu.SMEM((count,), jnp.int32),
            pltpu.VMEM(tokens.shape, BF16),
            pltpu.VMEM(kv_cache.shape, BF16),
            pltpu.VMEM(w_qkv.shape, BF16),
            pltpu.VMEM(w_o.shape, BF16),
            pltpu.VMEM((n, *w_in.shape), BF16),
            pltpu.VMEM((n, *w_down.shape), BF16),
            pltpu.VMEM(tokens.shape, BF16),
            pltpu.VMEM((count, new_len, hd), BF16),
            pltpu.VMEM((count, new_len, hd), BF16),
            pltpu.VMEM((count, n, tall, rows), BF16),
            pltpu.VMEM((count, n, tall, rows), BF16),
            pltpu.VMEM((count, n, tall, rows), BF16),
            pltpu.VMEM((count, n, tall, rows), BF16),
            pltpu.VMEM((count, rows, width), BF16),
            pltpu.VMEM((16, new_len), F32),
            dma((6,)),
            dma((2, n)),
            dma((2, n)),
            dma((count,)),
            dma((count,)),
            dma((count, n)),
            dma((count, n)),
            dma((count, n)),
            dma((count, n)),
        ],
        compiler_params=pltpu.CompilerParams(collective_id=0, has_side_effects=True, vmem_limit_bytes=VMEM_BYTES),
        name="layer",
    )(partner, cache_age, slope, tokens, kv_cache, w_qkv, w_o, attn_gain[None], mlp_gain[None], w_in, w_down)


def solution(mesh):
    in_specs = (
        P("qubit", None, None),
        P("qubit", "head", None, None),
        P("qubit", None),
        P("qubit"),
        P("head"),
        P(None, None, "head"),
        P(),
        P(),
        P(),
        P(None, "head"),
        P("head", None),
    )
    return jax.shard_map(
        functools.partial(on_device, mesh.shape["qubit"], mesh.shape["head"]),
        mesh=mesh,
        in_specs=in_specs,
        out_specs=P("qubit", "head", None),
        check_vma=False,
    )
```

profile of v0, /device:TPU:1, one launch (start us, length us, event | category | flops | bytes accessed | tf_op | source)
XLA Modules:
  0.0 106.8 jit_solution(17288667287507662778)
XLA Ops:
  0.0 1.3 %copy.12.age_ref = s32[8,3]{1,0:T(8,128)} copy(s32[8,3]{0,1:T(4,128)} %param.13) | data formatting | bytes 192 | tf_op args[2]
  1.3 103.1 %layer.1 = bf16[8,128,512]{2,1,0:T(8,128)(2,1)} custom-call(s32[8]{0:T(128)} %partner_ref.1, s32[8,3]{1,0:T(8,128)} %copy.12.age_ref, f32[4]{0:T(128)} %slope_ref.1, bf16[8,256,512]{2,1,0:T(8,128)(2,1)} %tokens_hbm.1, bf16[8,4,384,128]{3,2,1,0:T(8,128)(2,1)} %cache_hbm.1, bf16[3,512,256]{2,1,0:T(8,128)(2,1)} %w_qkv_hbm.1, bf16[512,512]{1,0:T(8,128)(2,1)} %w_o_hbm.1, ...), custom_call_target="tpu_custom_call" | custom-call | tf_op jit(solution)/shard_map/layer/pallas_call | solution.py:350
  104.5 2.3 %copy.14 = bf16[8,128,512]{2,1,0:T(8,128)(2,1)} copy(bf16[8,128,512]{2,1,0:T(8,128)(2,1)} %layer.1) | data formatting | bytes 2097152
where the time goes:
time: 107 us
  Pallas kernels  103 us (96%)
  local copies, waits for them, and re-layouts  3.61 us (3%)
    pallas_call x1, Pallas kernels, on_device(): pl.pallas_call(functools.partial(layer_kernel, n_dev), in_specs=[SMEM_SPE...  103 us
    unnamed x2, local copies, waits for them, and re-layouts  3.61 us

commit v1 on v0

--- a/solution.py
+++ b/solution.py
@@ -86,6 +86,8 @@
     n_all,
     f_send,
     f_recv,
+    l_send,
+    l_recv,
     result,
     lse_scr,
     load_sem,
@@ -97,6 +99,8 @@
     n_rs,
     f_ss,
     f_rs,
+    l_ss,
+    l_rs,
 ):
     count, new_len, _ = tok.shape
     heads, keys = cache.shape[1], cache.shape[2]
@@ -174,25 +178,33 @@
             device_id_type=MESH,
         )
 
-    def f_copy(c, t):
-        return pltpu.make_async_remote_copy(
-            src_ref=f_send.at[c, t],
-            dst_ref=f_recv.at[c, y],
-            send_sem=f_ss.at[c, t],
-            recv_sem=f_rs.at[c, y],
-            device_id=(mate(c), t),
-            device_id_type=MESH,
-        )
-
-    def f_arrival(c, group):
-        return pltpu.make_async_remote_copy(
-            src_ref=f_send.at[c, 0],
-            dst_ref=f_recv.at[c, group],
-            send_sem=f_ss.at[c, 0],
-            recv_sem=f_rs.at[c, group],
-            device_id=(mate(c), group),
-            device_id_type=MESH,
-        )
+    far_pairs = ((f_send, f_recv, f_ss, f_rs), (l_send, l_recv, l_ss, l_rs))
+
+    def f_copies(c, t):
+        return [
+            pltpu.make_async_remote_copy(
+                src_ref=src.at[c, t],
+                dst_ref=dst.at[c, y],
+                send_sem=ss.at[c, t],
+                recv_sem=rs.at[c, y],
+                device_id=(mate(c), t),
+                device_id_type=MESH,
+            )
+            for src, dst, ss, rs in far_pairs
+        ]
+
+    def f_arrivals(c, group):
+        return [
+            pltpu.make_async_remote_copy(
+                src_ref=src.at[c, 0],
+                dst_ref=dst.at[c, group],
+                send_sem=ss.at[c, 0],
+                recv_sem=rs.at[c, group],
+                device_id=(mate(c), group),
+                device_id_type=MESH,
+            )
+            for src, dst, ss, rs in far_pairs
+        ]
 
     def w_copy(i, r, src, dst):
         return pltpu.make_async_remote_copy(
@@ -235,7 +247,7 @@
 
     def cache_part(row, h):
         kv = cache[row, h]
-        biases = [-slope_ref[h] * age_ref[row, r].astype(F32) for r in range(rounds)]
+        biases = [-slope_ref[h] * age_ref[r, row].astype(F32) for r in range(rounds)]
         return kv[:, :DH], kv[:, DH:], biases, [0] * rounds
 
     def note_lse(h, lse):
@@ -275,8 +287,8 @@
             cols = slice(h * DH, (h + 1) * DH)
             out, lse = head_attention(q_recv[c, :, cols], [cache_part(row, h)])
             put(f_send, c, cols, out)
-            note_lse(h, lse)
-        put(f_send, c, slice(hd, None), lse_scr[...])
+            for t in range(n):
+                l_send[c, t, h : h + 1, :] = lse[:, t * rows : (t + 1) * rows]
 
     def attend_loop(c, _):
         near(c)
@@ -285,7 +297,8 @@
         q_copy(c).wait_recv()
         far(c)
         for t in range(n):
-            f_copy(c, t).start()
+            for copy in f_copies(c, t):
+                copy.start()
         return 0
 
     lax.fori_loop(0, count, attend_loop, 0)
@@ -304,9 +317,10 @@
             n_arrival(c, r).wait_recv()
         feats = []
         for group in range(n):
-            f_arrival(c, group).wait_recv()
+            for copy in f_arrivals(c, group):
+                copy.wait_recv()
             near_part, far_part = n_all[c, group], f_recv[c, group]
-            lse_near, lse_far = lse_of(near_part), lse_of(far_part)
+            lse_near, lse_far = lse_of(near_part), l_recv[c, group]
             top = jnp.maximum(lse_near, lse_far)
             a, b = jnp.exp(lse_near - top), jnp.exp(lse_far - top)
             a, b = a / (a + b), b / (a + b)
@@ -334,7 +348,8 @@
         for r in range(1, n):
             n_copy(c, r).wait_send()
         for t in range(n):
-            f_copy(c, t).wait_send()
+            for copy in f_copies(c, t):
+                copy.wait_send()
         return 0
 
     lax.fori_loop(0, count, drain_loop, 0)
@@ -366,8 +381,10 @@
             pltpu.VMEM((count, new_len, hd), BF16),
             pltpu.VMEM((count, n, tall, rows), BF16),
             pltpu.VMEM((count, n, tall, rows), BF16),
-            pltpu.VMEM((count, n, tall, rows), BF16),
-            pltpu.VMEM((count, n, tall, rows), BF16),
+            pltpu.VMEM((count, n, hd, rows), BF16),
+            pltpu.VMEM((count, n, hd, rows), BF16),
+            pltpu.VMEM((count, n, heads, rows), F32),
+            pltpu.VMEM((count, n, heads, rows), F32),
             pltpu.VMEM((count, rows, width), BF16),
             pltpu.VMEM((16, new_len), F32),
             dma((6,)),
@@ -379,10 +396,12 @@
             dma((count, n)),
             dma((count, n)),
             dma((count, n)),
+            dma((count, n)),
+            dma((count, n)),
         ],
         compiler_params=pltpu.CompilerParams(collective_id=0, has_side_effects=True, vmem_limit_bytes=VMEM_BYTES),
         name="layer",
-    )(partner, cache_age, slope, tokens, kv_cache, w_qkv, w_o, attn_gain[None], mlp_gain[None], w_in, w_down)
+    )(partner, cache_age.T, slope, tokens, kv_cache, w_qkv, w_o, attn_gain[None], mlp_gain[None], w_in, w_down)
 
 
 def solution(mesh):

time: 107 us -> 104 us (0.972)
  local copies, waits for them, and re-layouts: 3.61 us -> 2.26 us
    unnamed x2 -> x1, local copies, waits for them, and re-layouts: 3.61 us -> 2.26 us
    pallas_call x1, Pallas kernels: 103 us -> 102 us  [on_device(): pl.pallas_call(functools.partial(layer_kernel, n_dev), in_specs=[SMEM_SPE...]
where the time goes in v1:
time: 104 us
  Pallas kernels  102 us (98%)
  local copies, waits for them, and re-layouts  2.26 us (2%)
    pallas_call x1, Pallas kernels, on_device(): pl.pallas_call(functools.partial(layer_kernel, n_dev), in_specs=[SMEM_SPE...  102 us
    unnamed x1, local copies, waits for them, and re-layouts  2.26 us

profile of v1, /device:TPU:1, one launch (start us, length us, event | category | flops | bytes accessed | tf_op | source)
XLA Modules:
  0.0 104.3 jit_solution(5284123116040980031)
XLA Ops:
  0.0 102.0 %layer.1 = bf16[8,128,512]{2,1,0:T(8,128)(2,1)} custom-call(s32[8]{0:T(128)} %partner_ref.1, s32[3,8]{1,0:T(4,128)} %bitcast.3, f32[4]{0:T(128)} %slope_ref.1, bf16[8,256,512]{2,1,0:T(8,128)(2,1)} %tokens_hbm.1, bf16[8,4,384,128]{3,2,1,0:T(8,128)(2,1)} %cache_hbm.1, bf16[3,512,256]{2,1,0:T(8,128)(2,1)} %w_qkv_hbm.1, bf16[512,512]{1,0:T(8,128)(2,1)} %w_o_hbm.1, ...), custom_call_target="tpu_custom_call" | custom-call | tf_op jit(solution)/shard_map/layer/pallas_call | solution.py:365
  102.0 2.3 %copy.13 = bf16[8,128,512]{2,1,0:T(8,128)(2,1)} copy(bf16[8,128,512]{2,1,0:T(8,128)(2,1)} %layer.1) | data formatting | bytes 2097152
